TPU v7x, 32 devices: a whole 2x2x4 slice. The times are simulated.
32 devices in a mesh: chan: 8 (over z, x), src: 4 (over y, core).
Axes of the slice: x: 2, y: 2, z: 4, core: 2. Of those that a mesh axis runs over, the one named last changes fastest.
Arguments:
- records: bfloat16 [1024, 4096], P('chan'), may hold values from -600 to 600
- virtual_sources: int32 [64], P('src'), may hold values from 0 to 1023
- pair_group: int32 [4096, 1], P(('chan', 'src')), may hold values from 0 to 7; in each aligned block of 128 rows (0 to 127, 128 to 255, ...) at most 32 rows name the same one
- pair_receiver: int32 [4096], P(('chan', 'src')), may hold values from 0 to 127
- pair_source: int32 [4096], P(('chan', 'src')), may hold values from 0 to 15
- observed: float32 [4096, 2048], P(('chan', 'src')), may hold values from -6 to 6
Outputs:
- adjoint_source: float32 [1024, 4096], P(('chan', 'src'))
- pair_misfit: float32 [4096], P(('chan', 'src'))
Inputs may be any that keep to these rules, and one draw needn't show every extreme that they name: `pair_group`: among the 128 pairs listed by one device at most 32 name the same channel group, and in every draw some device lists exactly 32 pairs for some group.
All inputs are finite; a program needn't handle non-finite values.
Results may differ from a plain program's by a relative error of at most 0.0021.
Values sent between devices are 32-bit elements; how exact they have to be, the bound alone decides.
No kernel may reach another device: no remote copies, remote signals or barrier semaphores. Data moves between devices by JAX's collectives and lax.ppermute only.
A program may use at most 64 MiB of HBM per device.

v0:
```python
import math
import jax
import jax.numpy as jnp
from jax import lax
from jax.sharding import PartitionSpec as P

K0 = 64


def fourier_basis(offset, length, time_len, bin_count):
    sample_times = offset + jnp.arange(length, dtype=jnp.int32)[:, None]
    band_bins = K0 + jnp.arange(bin_count, dtype=jnp.int32)[None, :]
    phase_index = band_bins * sample_times % (2 * time_len)
    angles = phase_index.astype(jnp.float32) * (math.pi / time_len)
    return jnp.concatenate([jnp.cos(angles), -jnp.sin(angles)], axis=1)


def forward(signal_rows, bin_count):
    time_len = signal_rows.shape[1]
    block_len = min(512, time_len)

    def add_block(block_index, running):
        offset = block_index * block_len
        segment = lax.dynamic_slice_in_dim(signal_rows, offset, block_len, 1)
        fourier_table = fourier_basis(offset, block_len, time_len, bin_count).astype(jnp.bfloat16)
        return running + jnp.dot(segment, fourier_table, preferred_element_type=jnp.float32)

    return lax.fori_loop(
        0,
        time_len // block_len,
        add_block,
        jnp.zeros((signal_rows.shape[0], 2 * bin_count), jnp.float32),
    )


def inverse(spectral, time_len):
    bin_count = spectral.shape[1] // 2
    block_len = min(512, time_len)

    def fill_block(block_index, output):
        offset = block_index * block_len
        fourier_table = fourier_basis(offset, block_len, time_len, bin_count)
        values = lax.dot_general(
            spectral,
            fourier_table,
            (((1,), (1,)), ((), ())),
            precision=lax.Precision.HIGHEST,
            preferred_element_type=jnp.float32,
        ) * (1.0 / math.sqrt(bin_count))
        return lax.dynamic_update_slice_in_dim(output, values, offset, 1)

    return lax.fori_loop(
        0, time_len // block_len, fill_block, jnp.zeros((spectral.shape[0], time_len), jnp.float32)
    )


def whiten(spectra):
    bin_count = spectra.shape[1] // 2
    band_power = jnp.sum(spectra * spectra, axis=1, keepdims=True) / bin_count
    return spectra / jnp.sqrt(band_power + 1e-06)


def band_taper(bin_count):
    band_bins = jnp.arange(bin_count, dtype=jnp.int32).astype(jnp.float32)
    return 0.5 - 0.5 * jnp.cos((band_bins + 0.5) * (2.0 * math.pi / bin_count))


def pair_terms(source_rows, receiver_rows, observed_rows):
    bin_count = observed_rows.shape[-1] // 2
    weights = band_taper(bin_count)
    source_real = source_rows[..., :bin_count]
    source_imag = source_rows[..., bin_count:]
    receiver_real = receiver_rows[..., :bin_count]
    receiver_imag = receiver_rows[..., bin_count:]
    corr_real = source_real * receiver_real + source_imag * receiver_imag
    corr_imag = source_real * receiver_imag - source_imag * receiver_real
    diff_real = corr_real - observed_rows[..., :bin_count]
    diff_imag = corr_imag - observed_rows[..., bin_count:]
    misfit = jnp.sum(weights * (diff_real * diff_real + diff_imag * diff_imag), axis=-1) / (
        2 * bin_count
    )
    resid_real = weights * diff_real
    resid_imag = weights * diff_imag
    term_real = resid_real * source_real - resid_imag * source_imag
    term_imag = resid_real * source_imag + resid_imag * source_real
    return (misfit, jnp.concatenate([term_real, term_imag], axis=-1))


def per_device(records, virtual_sources, pair_group, pair_receiver, pair_source, observed):
    row_count, time_len = records.shape
    pair_count = observed.shape[0]
    bin_count = observed.shape[1] // 2
    groups = lax.axis_size("chan")
    capacity = 2 * pair_count // groups
    slot_total = groups * capacity
    chan_index = lax.axis_index("chan")
    local_rows = virtual_sources - chan_index * row_count
    inside = (local_rows >= 0) & (local_rows < row_count)
    safe_rows = jnp.clip(local_rows, 0, row_count - 1)
    whitened = whiten(forward(records, bin_count))
    picked = jnp.where(inside[:, None], jnp.take(whitened, safe_rows, axis=0), 0.0)
    sources = lax.psum(picked, "chan")
    destination = pair_group[:, 0]
    group_hits = (destination[:, None] == jnp.arange(groups, dtype=jnp.int32)[None, :]).astype(
        jnp.int32
    )
    slot_ranks = jnp.sum((jnp.cumsum(group_hits, axis=0) - 1) * group_hits, axis=1)
    slot_index = destination * capacity + slot_ranks
    send_receiver = (
        jnp.full((slot_total,), -1, jnp.int32)
        .at[slot_index]
        .set(pair_receiver)
        .reshape(groups, capacity)
    )
    send_source = (
        jnp.zeros((slot_total,), jnp.int32)
        .at[slot_index]
        .set(pair_source)
        .reshape(groups, capacity)
    )
    send_labels = jnp.stack([send_receiver, send_source], axis=-1)
    send_observed = (
        jnp.zeros((slot_total, 2 * bin_count), jnp.float32)
        .at[slot_index]
        .set(observed)
        .reshape(groups, capacity, 2 * bin_count)
    )
    observed_slots = lax.all_to_all(send_observed, "chan", split_axis=0, concat_axis=0, tiled=True)
    label_slots = lax.all_to_all(send_labels, "chan", split_axis=0, concat_axis=0, tiled=True)
    receiver_slots = label_slots[..., 0]
    source_slots = label_slots[..., 1]
    occupied = receiver_slots >= 0
    receiver_rows = jnp.take(whitened, jnp.clip(receiver_slots, 0, row_count - 1), axis=0)
    source_rows = jnp.take(sources, jnp.clip(source_slots, 0, sources.shape[0] - 1), axis=0)
    misfit, adjoint_term = pair_terms(source_rows, receiver_rows, observed_slots)
    adjoint_term = jnp.where(occupied[..., None], adjoint_term, 0.0)
    returned = lax.all_to_all(misfit, "chan", split_axis=0, concat_axis=0, tiled=True)
    arrived_terms, receivers, returned = (adjoint_term, receiver_slots, returned)
    pair_misfit = returned.reshape(slot_total)[slot_index]
    flat_terms = arrived_terms.reshape(slot_total, 2 * bin_count)
    flat_receivers = receivers.reshape(slot_total)
    selector = (jnp.arange(row_count, dtype=jnp.int32)[:, None] == flat_receivers[None, :]).astype(
        jnp.float32
    )
    adjoint_spectra = jnp.dot(
        selector, flat_terms, precision=lax.Precision.HIGHEST, preferred_element_type=jnp.float32
    )
    adjoint_source = lax.psum_scatter(
        inverse(adjoint_spectra, time_len), "src", scatter_dimension=0, tiled=True
    )
    return (adjoint_source, pair_misfit)


def solution(mesh):
    return jax.shard_map(
        per_device,
        mesh=mesh,
        in_specs=(
            P("chan", None),
            P("src"),
            P(("chan", "src"), None),
            P(("chan", "src")),
            P(("chan", "src")),
            P(("chan", "src"), None),
        ),
        out_specs=(P(("chan", "src"), None), P(("chan", "src"))),
        check_vma=False,
    )
```

profile of v0, /device:TPU:0, one launch (start us, length us, event | category | flops | bytes accessed | tf_op | source)
XLA Modules:
  0.0 358.6 jit_solution(7600043194722808114)
XLA Ops:
  12.6 7.3 %all-to-all-start = ((s32[8,32,2]{1,2,0:T(2,128)}), s32[8,32,2]{1,2,0:T(2,128)S(1)}, u32[]{:S(2)}, u32[]{:S(2)}) async-start(s32[8,32,2]{1,2,0:T(2,128)} %pad_add_fusion), calls=%async_computation | async-start | bytes 16384 | tf_op jit(solution)/shard_map/all_to_all | solution.py:129
  19.9 84.7 %while.32 = (s32[]{:T(128)}, f32[128,2048]{1,0:T(8,128)S(1)}, bf16[128,4096]{1,0:T(8,128)(2,1)}, s32[]{:T(128)}, s32[]{:T(128)}, /*index=5*/s32[]{:T(128)}, s32[]{:T(128)}) while((s32[]{:T(128)}, f32[128,2048]{1,0:T(8,128)S(1)}, bf16[128,4096]{1,0:T(8,128)(2,1)}, s32[]{:T(128)}, s32[]{:T(128)}, /*index=5*/s32[]{:T(128)}, ...), condition=%wide.region_5.6_spmd.clone, body=%wide.region_4.5_spmd.clone.sunk | while | flops 282068480 | bytes 6434957 | solution.py:28
  19.9 9.0 %cosine_convert_fusion.2 = (bf16[512,1024]{1,0:T(8,128)(2,1)S(1)}, bf16[512,1024]{1,0:T(8,128)(2,1)S(1)}) fusion(s32[512]{0:T(512)S(1)} %iota_add_fusion.10, s32[1024]{0:T(1024)S(1)} %iota_add_fusion.11), kind=kLoop, calls=%fused_computation.40.clone.1 | loop fusion | flops 8912896 | bytes 2103296 | tf_op jit(solution)/shard_map/convert
  30.5 9.0 %cosine_convert_fusion.2 = (bf16[512,1024]{1,0:T(8,128)(2,1)S(1)}, bf16[512,1024]{1,0:T(8,128)(2,1)S(1)}) fusion(s32[512]{0:T(512)S(1)} %iota_add_fusion.10, s32[1024]{0:T(1024)S(1)} %iota_add_fusion.11), kind=kLoop, calls=%fused_computation.40.clone.1 | loop fusion | flops 8912896 | bytes 2103296 | tf_op jit(solution)/shard_map/convert
  41.1 9.0 %cosine_convert_fusion.2 = (bf16[512,1024]{1,0:T(8,128)(2,1)S(1)}, bf16[512,1024]{1,0:T(8,128)(2,1)S(1)}) fusion(s32[512]{0:T(512)S(1)} %iota_add_fusion.10, s32[1024]{0:T(1024)S(1)} %iota_add_fusion.11), kind=kLoop, calls=%fused_computation.40.clone.1 | loop fusion | flops 8912896 | bytes 2103296 | tf_op jit(solution)/shard_map/convert
  51.7 9.0 %cosine_convert_fusion.2 = (bf16[512,1024]{1,0:T(8,128)(2,1)S(1)}, bf16[512,1024]{1,0:T(8,128)(2,1)S(1)}) fusion(s32[512]{0:T(512)S(1)} %iota_add_fusion.10, s32[1024]{0:T(1024)S(1)} %iota_add_fusion.11), kind=kLoop, calls=%fused_computation.40.clone.1 | loop fusion | flops 8912896 | bytes 2103296 | tf_op jit(solution)/shard_map/convert
  62.2 9.0 %cosine_convert_fusion.2 = (bf16[512,1024]{1,0:T(8,128)(2,1)S(1)}, bf16[512,1024]{1,0:T(8,128)(2,1)S(1)}) fusion(s32[512]{0:T(512)S(1)} %iota_add_fusion.10, s32[1024]{0:T(1024)S(1)} %iota_add_fusion.11), kind=kLoop, calls=%fused_computation.40.clone.1 | loop fusion | flops 8912896 | bytes 2103296 | tf_op jit(solution)/shard_map/convert
  72.8 9.0 %cosine_convert_fusion.2 = (bf16[512,1024]{1,0:T(8,128)(2,1)S(1)}, bf16[512,1024]{1,0:T(8,128)(2,1)S(1)}) fusion(s32[512]{0:T(512)S(1)} %iota_add_fusion.10, s32[1024]{0:T(1024)S(1)} %iota_add_fusion.11), kind=kLoop, calls=%fused_computation.40.clone.1 | loop fusion | flops 8912896 | bytes 2103296 | tf_op jit(solution)/shard_map/convert
  83.4 9.0 %cosine_convert_fusion.2 = (bf16[512,1024]{1,0:T(8,128)(2,1)S(1)}, bf16[512,1024]{1,0:T(8,128)(2,1)S(1)}) fusion(s32[512]{0:T(512)S(1)} %iota_add_fusion.10, s32[1024]{0:T(1024)S(1)} %iota_add_fusion.11), kind=kLoop, calls=%fused_computation.40.clone.1 | loop fusion | flops 8912896 | bytes 2103296 | tf_op jit(solution)/shard_map/convert
  94.0 9.0 %cosine_convert_fusion.2 = (bf16[512,1024]{1,0:T(8,128)(2,1)S(1)}, bf16[512,1024]{1,0:T(8,128)(2,1)S(1)}) fusion(s32[512]{0:T(512)S(1)} %iota_add_fusion.10, s32[1024]{0:T(1024)S(1)} %iota_add_fusion.11), kind=kLoop, calls=%fused_computation.40.clone.1 | loop fusion | flops 8912896 | bytes 2103296 | tf_op jit(solution)/shard_map/convert
  107.9 6.1 %all-to-all-start.1 = ((f32[8,32,2048]{2,1,0:T(8,128)}), f32[8,32,2048]{2,1,0:T(8,128)}, u32[]{:S(2)}, u32[]{:S(2)}) async-start(f32[8,32,2048]{2,1,0:T(8,128)} %bitcast.8), calls=%async_computation.1 | async-start | bytes 4194304 | tf_op jit(solution)/shard_map/all_to_all | solution.py:128
  119.0 87.0 %all-reduce.2.cloned.1.call-done = f32[16,2048]{1,0:T(8,128)} async-done(((f32[16,2048]{1,0:T(8,128)}), f32[16,2048]{1,0:T(8,128)}) %all-reduce.2.cloned.1.call-update) | async-done | bytes 131088 | tf_op jit(solution)/shard_map/psum | solution.py:102
  206.0 4.6 %gather_fusion.1 = f32[256,2048]{1,0:T(8,128)} fusion(f32[16,2048]{1,0:T(8,128)} %all-reduce.2.cloned.1.call-done, s32[1024]{0:T(1024)S(1)} %pad_clamp_fusion.2), kind=kCustom, calls=%fused_computation.1 | custom fusion | bytes 4195328 | tf_op jit(solution)/shard_map/jit(_take)/gather | solution.py:134
  220.2 101.1 %while.31 = (s32[]{:T(128)}, f32[128,4096]{1,0:T(8,128)}, f32[128,2048]{1,0:T(8,128)S(1)}, s32[]{:T(128)}, s32[]{:T(128)}, /*index=5*/s32[]{:T(128)}, s32[]{:T(128)}) while((s32[]{:T(128)}, f32[128,4096]{1,0:T(8,128)}, f32[128,2048]{1,0:T(8,128)S(1)}, s32[]{:T(128)}, s32[]{:T(128)}, /*index=5*/s32[]{:T(128)}, s32[]{:T(128)}) %tuple.92), condition=%wide.region_10.11_spmd, body=%wide.region_9.10_spmd.sunk | while | flops 1619592704 | bytes 10760323 | solution.py:52
  220.2 8.3 %fusion.50 = (f32[512,1024]{1,0:T(8,128)S(1)}, f32[512,1024]{1,0:T(8,128)S(1)}) fusion(s32[512]{0:T(512)S(1)} %iota_add_fusion.8, s32[1024]{0:T(1024)S(1)} %iota_add_fusion.9), kind=kLoop, calls=%fused_computation.22.clone.1 | loop fusion | flops 7864320 | bytes 4200448 | tf_op jit(solution)/shard_map/while/body/eval_jaxpr/cos | solution.py:15
  232.9 8.3 %fusion.50 = (f32[512,1024]{1,0:T(8,128)S(1)}, f32[512,1024]{1,0:T(8,128)S(1)}) fusion(s32[512]{0:T(512)S(1)} %iota_add_fusion.8, s32[1024]{0:T(1024)S(1)} %iota_add_fusion.9), kind=kLoop, calls=%fused_computation.22.clone.1 | loop fusion | flops 7864320 | bytes 4200448 | tf_op jit(solution)/shard_map/while/body/eval_jaxpr/cos | solution.py:15
  245.5 8.3 %fusion.50 = (f32[512,1024]{1,0:T(8,128)S(1)}, f32[512,1024]{1,0:T(8,128)S(1)}) fusion(s32[512]{0:T(512)S(1)} %iota_add_fusion.8, s32[1024]{0:T(1024)S(1)} %iota_add_fusion.9), kind=kLoop, calls=%fused_computation.22.clone.1 | loop fusion | flops 7864320 | bytes 4200448 | tf_op jit(solution)/shard_map/while/body/eval_jaxpr/cos | solution.py:15
  258.2 8.3 %fusion.50 = (f32[512,1024]{1,0:T(8,128)S(1)}, f32[512,1024]{1,0:T(8,128)S(1)}) fusion(s32[512]{0:T(512)S(1)} %iota_add_fusion.8, s32[1024]{0:T(1024)S(1)} %iota_add_fusion.9), kind=kLoop, calls=%fused_computation.22.clone.1 | loop fusion | flops 7864320 | bytes 4200448 | tf_op jit(solution)/shard_map/while/body/eval_jaxpr/cos | solution.py:15
  270.8 8.3 %fusion.50 = (f32[512,1024]{1,0:T(8,128)S(1)}, f32[512,1024]{1,0:T(8,128)S(1)}) fusion(s32[512]{0:T(512)S(1)} %iota_add_fusion.8, s32[1024]{0:T(1024)S(1)} %iota_add_fusion.9), kind=kLoop, calls=%fused_computation.22.clone.1 | loop fusion | flops 7864320 | bytes 4200448 | tf_op jit(solution)/shard_map/while/body/eval_jaxpr/cos | solution.py:15
  283.4 8.3 %fusion.50 = (f32[512,1024]{1,0:T(8,128)S(1)}, f32[512,1024]{1,0:T(8,128)S(1)}) fusion(s32[512]{0:T(512)S(1)} %iota_add_fusion.8, s32[1024]{0:T(1024)S(1)} %iota_add_fusion.9), kind=kLoop, calls=%fused_computation.22.clone.1 | loop fusion | flops 7864320 | bytes 4200448 | tf_op jit(solution)/shard_map/while/body/eval_jaxpr/cos | solution.py:15
  296.1 8.3 %fusion.50 = (f32[512,1024]{1,0:T(8,128)S(1)}, f32[512,1024]{1,0:T(8,128)S(1)}) fusion(s32[512]{0:T(512)S(1)} %iota_add_fusion.8, s32[1024]{0:T(1024)S(1)} %iota_add_fusion.9), kind=kLoop, calls=%fused_computation.22.clone.1 | loop fusion | flops 7864320 | bytes 4200448 | tf_op jit(solution)/shard_map/while/body/eval_jaxpr/cos | solution.py:15
  308.7 8.3 %fusion.50 = (f32[512,1024]{1,0:T(8,128)S(1)}, f32[512,1024]{1,0:T(8,128)S(1)}) fusion(s32[512]{0:T(512)S(1)} %iota_add_fusion.8, s32[1024]{0:T(1024)S(1)} %iota_add_fusion.9), kind=kLoop, calls=%fused_computation.22.clone.1 | loop fusion | flops 7864320 | bytes 4200448 | tf_op jit(solution)/shard_map/while/body/eval_jaxpr/cos | solution.py:15
  325.7 6.5 %all-to-all-done.2 = f32[8,1,32]{2,1,0:T(1,128)S(1)} async-done(((f32[8,1,32]{2,1,0:T(1,128)}), f32[8,1,32]{2,1,0:T(1,128)S(1)}, u32[]{:S(2)}, u32[]{:S(2)}) %all-to-all-start.2) | async-done | bytes 1056 | tf_op jit(solution)/shard_map/all_to_all | solution.py:137
  335.2 16.6 %reduce-scatter.2.cloned.1.call-done = f32[32,4096]{1,0:T(8,128)} async-done(((f32[128,4096]{1,0:T(8,128)}), f32[32,4096]{1,0:T(8,128)}) %reduce-scatter.2.cloned.1.call-update) | async-done | bytes 524304 | tf_op jit(solution)/shard_map/reduce_scatter | solution.py:148
  (115 shorter events, 77.1 us)
Async XLA Ops:
  12.6 95.3 %all-to-all-start = ((s32[8,32,2]{1,2,0:T(2,128)}), s32[8,32,2]{1,2,0:T(2,128)S(1)}, u32[]{:S(2)}, u32[]{:S(2)}) async-start(s32[8,32,2]{1,2,0:T(2,128)} %pad_add_fusion), calls=%async_computation | async-start | bytes 16384 | tf_op jit(solution)/shard_map/all_to_all | solution.py:129
  107.9 6.2 %copy-start = (s32[16]{0:T(128)S(1)}, s32[16]{0:T(128)}, u32[]{:S(2)}) copy-start(s32[16]{0:T(128)} %param.11) | copy-start | bytes 196
  107.9 106.6 %all-to-all-start.1 = ((f32[8,32,2048]{2,1,0:T(8,128)}), f32[8,32,2048]{2,1,0:T(8,128)}, u32[]{:S(2)}, u32[]{:S(2)}) async-start(f32[8,32,2048]{2,1,0:T(8,128)} %bitcast.8), calls=%async_computation.1 | async-start | bytes 4194304 | tf_op jit(solution)/shard_map/all_to_all | solution.py:128
  114.0 92.0 %all-reduce.2.cloned.1.call-start = ((), (), s32[]{:S(2)}) async-start(), calls=%async_computation.4 | async-start | bytes 262144 | tf_op jit(solution)/shard_map/psum | solution.py:102
  115.8 236.0 %reduce-scatter.2.cloned.1.call-start = ((), (), s32[]{:S(2)}) async-start(), calls=%async_computation.5 | async-start | bytes 2621440 | tf_op jit(solution)/shard_map/reduce_scatter | solution.py:148
  321.9 10.2 %all-to-all-start.2 = ((f32[8,1,32]{2,1,0:T(1,128)}), f32[8,1,32]{2,1,0:T(1,128)S(1)}, u32[]{:S(2)}, u32[]{:S(2)}) async-start(f32[8,1,32]{2,1,0:T(1,128)} %bitcast.11), calls=%async_computation.3 | async-start | bytes 8192 | tf_op jit(solution)/shard_map/all_to_all | solution.py:137
Sparse Core Ops, SparseCore 0:
  118.7 87.2 all-reduce.1
  321.5 30.2 reduce-scatter.1
where the time goes:
time: 359 us
  other arithmetic  151 us (42%)
  waiting for transfers between devices  110 us (31%)
  matrix products  40.4 us (11%)
  local copies, waits for them, and re-layouts  24.9 us (7%)
  starting transfers between devices  17.2 us (5%)
  between operations  14.2 us (4%)
    psum x1, waiting for transfers between devices, per_device(): sources = lax.psum(picked, 'chan')  87 us
    another operation x8, other arithmetic  72.2 us
    cos x8, other arithmetic, fourier_basis(): return jnp.concatenate([jnp.cos(angles), -jnp.sin(angles)], axis=1)  66.4 us
    dot_general x8, matrix products, fill_block(): lax.dot_general(spectral, fourier_table, (((1,), (1,)), ((), ())), precis...  27.4 us
    reduce_scatter x1, waiting for transfers between devices, per_device(): lax.psum_scatter(inverse(adjoint_spectra, time_len), 'src', scatter_dimen...  16.6 us
    dot_general x8, matrix products, add_block(): jnp.dot(segment, fourier_table, preferred_element_type=jnp.float32)  12 us
    all_to_all x1, starting transfers between devices, per_device(): lax.all_to_all(send_labels, 'chan', split_axis=0, concat_axis=0, tiled=True)  7.28 us
  transfers between devices with their start and end apart: 5, of which 3 were waited for; matrix products, arithmetic and copies ran while one was open for 29% of the time, Pallas kernels for 0%

commit v1 on v0

--- a/solution.py
+++ b/solution.py
@@ -99,7 +99,9 @@
     safe_rows = jnp.clip(local_rows, 0, row_count - 1)
     whitened = whiten(forward(records, bin_count))
     picked = jnp.where(inside[:, None], jnp.take(whitened, safe_rows, axis=0), 0.0)
-    sources = lax.psum(picked, "chan")
+    sources = picked
+    for hop in (1, 2, 4):
+        sources = sources + lax.ppermute(sources, "chan", [(dev, dev ^ hop) for dev in range(8)])
     destination = pair_group[:, 0]
     group_hits = (destination[:, None] == jnp.arange(groups, dtype=jnp.int32)[None, :]).astype(
         jnp.int32

time: 359 us -> 319 us (0.89)
  waiting for transfers between devices: 110 us -> 65.4 us
  starting transfers between devices: 17.2 us -> 23.8 us
    psum x1 -> x0, waiting for transfers between devices: 87 us -> none  [per_device(): sources = lax.psum(picked, 'chan')]
    ppermute x0 -> x3, waiting for transfers between devices: none -> 42.2 us  [per_device(): lax.ppermute(sources, 'chan', [(dev, dev ^ hop) for dev in range(8)])]
    ppermute x0 -> x3, starting transfers between devices: none -> 6.87 us  [per_device(): lax.ppermute(sources, 'chan', [(dev, dev ^ hop) for dev in range(8)])]
  transfers between devices with their start and end apart: 5 -> 7, of which waited for: 3 -> 5; matrix products, arithmetic and copies ran while one was open for 29% -> 32% of each run, Pallas kernels for 0% -> 0%
where the time goes in v1:
time: 319 us; the launch traced here: 318 us
  other arithmetic  151 us (47%)
  waiting for transfers between devices  65.4 us (21%)
  matrix products  40.4 us (13%)
  starting transfers between devices  23.8 us (7%)
  local copies, waits for them, and re-layouts  23 us (7%)
  between operations  14.2 us (4%)
    another operation x8, other arithmetic  72.2 us
    cos x8, other arithmetic, fourier_basis(): return jnp.concatenate([jnp.cos(angles), -jnp.sin(angles)], axis=1)  66.4 us
    ppermute x3, waiting for transfers between devices, per_device(): lax.ppermute(sources, 'chan', [(dev, dev ^ hop) for dev in range(8)])  42.2 us
    dot_general x8, matrix products, fill_block(): lax.dot_general(spectral, fourier_table, (((1,), (1,)), ((), ())), precis...  27.4 us
    reduce_scatter x1, waiting for transfers between devices, per_device(): lax.psum_scatter(inverse(adjoint_spectra, time_len), 'src', scatter_dimen...  16.6 us
    dot_general x8, matrix products, add_block(): jnp.dot(segment, fourier_table, preferred_element_type=jnp.float32)  12 us
    all_to_all x1, starting transfers between devices, per_device(): lax.all_to_all(send_labels, 'chan', split_axis=0, concat_axis=0, tiled=True)  7.28 us
    dynamic_update_slice x16, local copies, waits for them, and re-layouts, fill_block(): return lax.dynamic_update_slice_in_dim(output, values, offset, 1)  7.05 us
  transfers between devices with their start and end apart: 7, of which 5 were waited for; matrix products, arithmetic and copies ran while one was open for 32% of the time, Pallas kernels for 0%

profile of v1, /device:TPU:0, one launch (start us, length us, event | category | flops | bytes accessed | tf_op | source)
XLA Modules:
  0.0 318.1 jit_solution(5846212890814692909)
XLA Ops:
  12.6 7.3 %all-to-all-start = ((s32[8,32,2]{1,2,0:T(2,128)}), s32[8,32,2]{1,2,0:T(2,128)S(1)}, u32[]{:S(2)}, u32[]{:S(2)}) async-start(s32[8,32,2]{1,2,0:T(2,128)} %pad_add_fusion), calls=%async_computation | async-start | bytes 16384 | tf_op jit(solution)/shard_map/all_to_all | solution.py:131
  19.9 84.7 %while.32 = (s32[]{:T(128)}, f32[128,2048]{1,0:T(8,128)S(1)}, bf16[128,4096]{1,0:T(8,128)(2,1)}, s32[]{:T(128)}, s32[]{:T(128)}, /*index=5*/s32[]{:T(128)}, s32[]{:T(128)}) while((s32[]{:T(128)}, f32[128,2048]{1,0:T(8,128)S(1)}, bf16[128,4096]{1,0:T(8,128)(2,1)}, s32[]{:T(128)}, s32[]{:T(128)}, /*index=5*/s32[]{:T(128)}, ...), condition=%wide.region_5.6_spmd.clone, body=%wide.region_4.5_spmd.clone.sunk | while | flops 282068480 | bytes 6434957 | solution.py:28
  19.9 9.0 %cosine_convert_fusion.2 = (bf16[512,1024]{1,0:T(8,128)(2,1)S(1)}, bf16[512,1024]{1,0:T(8,128)(2,1)S(1)}) fusion(s32[512]{0:T(512)S(1)} %iota_add_fusion.10, s32[1024]{0:T(1024)S(1)} %iota_add_fusion.11), kind=kLoop, calls=%fused_computation.40.clone.1 | loop fusion | flops 8912896 | bytes 2103296 | tf_op jit(solution)/shard_map/convert
  30.5 9.0 %cosine_convert_fusion.2 = (bf16[512,1024]{1,0:T(8,128)(2,1)S(1)}, bf16[512,1024]{1,0:T(8,128)(2,1)S(1)}) fusion(s32[512]{0:T(512)S(1)} %iota_add_fusion.10, s32[1024]{0:T(1024)S(1)} %iota_add_fusion.11), kind=kLoop, calls=%fused_computation.40.clone.1 | loop fusion | flops 8912896 | bytes 2103296 | tf_op jit(solution)/shard_map/convert
  41.1 9.0 %cosine_convert_fusion.2 = (bf16[512,1024]{1,0:T(8,128)(2,1)S(1)}, bf16[512,1024]{1,0:T(8,128)(2,1)S(1)}) fusion(s32[512]{0:T(512)S(1)} %iota_add_fusion.10, s32[1024]{0:T(1024)S(1)} %iota_add_fusion.11), kind=kLoop, calls=%fused_computation.40.clone.1 | loop fusion | flops 8912896 | bytes 2103296 | tf_op jit(solution)/shard_map/convert
  51.7 9.0 %cosine_convert_fusion.2 = (bf16[512,1024]{1,0:T(8,128)(2,1)S(1)}, bf16[512,1024]{1,0:T(8,128)(2,1)S(1)}) fusion(s32[512]{0:T(512)S(1)} %iota_add_fusion.10, s32[1024]{0:T(1024)S(1)} %iota_add_fusion.11), kind=kLoop, calls=%fused_computation.40.clone.1 | loop fusion | flops 8912896 | bytes 2103296 | tf_op jit(solution)/shard_map/convert
  62.3 9.0 %cosine_convert_fusion.2 = (bf16[512,1024]{1,0:T(8,128)(2,1)S(1)}, bf16[512,1024]{1,0:T(8,128)(2,1)S(1)}) fusion(s32[512]{0:T(512)S(1)} %iota_add_fusion.10, s32[1024]{0:T(1024)S(1)} %iota_add_fusion.11), kind=kLoop, calls=%fused_computation.40.clone.1 | loop fusion | flops 8912896 | bytes 2103296 | tf_op jit(solution)/shard_map/convert
  72.8 9.0 %cosine_convert_fusion.2 = (bf16[512,1024]{1,0:T(8,128)(2,1)S(1)}, bf16[512,1024]{1,0:T(8,128)(2,1)S(1)}) fusion(s32[512]{0:T(512)S(1)} %iota_add_fusion.10, s32[1024]{0:T(1024)S(1)} %iota_add_fusion.11), kind=kLoop, calls=%fused_computation.40.clone.1 | loop fusion | flops 8912896 | bytes 2103296 | tf_op jit(solution)/shard_map/convert
  83.4 9.0 %cosine_convert_fusion.2 = (bf16[512,1024]{1,0:T(8,128)(2,1)S(1)}, bf16[512,1024]{1,0:T(8,128)(2,1)S(1)}) fusion(s32[512]{0:T(512)S(1)} %iota_add_fusion.10, s32[1024]{0:T(1024)S(1)} %iota_add_fusion.11), kind=kLoop, calls=%fused_computation.40.clone.1 | loop fusion | flops 8912896 | bytes 2103296 | tf_op jit(solution)/shard_map/convert
  94.0 9.0 %cosine_convert_fusion.2 = (bf16[512,1024]{1,0:T(8,128)(2,1)S(1)}, bf16[512,1024]{1,0:T(8,128)(2,1)S(1)}) fusion(s32[512]{0:T(512)S(1)} %iota_add_fusion.10, s32[1024]{0:T(1024)S(1)} %iota_add_fusion.11), kind=kLoop, calls=%fused_computation.40.clone.1 | loop fusion | flops 8912896 | bytes 2103296 | tf_op jit(solution)/shard_map/convert
  117.2 17.3 %collective-permute-done = f32[16,2048]{1,0:T(8,128)S(1)} collective-permute-done((f32[16,2048]{1,0:T(8,128)S(1)}, f32[16,2048]{1,0:T(8,128)S(1)}, u32[]{:S(2)}, u32[]{:S(2)}) %collective-permute-start) | collective-permute-done | bytes 131104 | tf_op jit(solution)/shard_map/ppermute | solution.py:104
  135.2 15.5 %collective-permute-done.1 = f32[16,2048]{1,0:T(8,128)S(1)} collective-permute-done((f32[16,2048]{1,0:T(8,128)S(1)}, f32[16,2048]{1,0:T(8,128)S(1)}, u32[]{:S(2)}, u32[]{:S(2)}) %collective-permute-start.1) | collective-permute-done | bytes 131104 | tf_op jit(solution)/shard_map/ppermute | solution.py:104
  157.9 9.4 %collective-permute-done.2 = f32[16,2048]{1,0:T(8,128)S(1)} collective-permute-done((f32[16,2048]{1,0:T(8,128)S(1)}, f32[16,2048]{1,0:T(8,128)S(1)}, u32[]{:S(2)}, u32[]{:S(2)}) %collective-permute-start.2) | collective-permute-done | bytes 131104 | tf_op jit(solution)/shard_map/ppermute | solution.py:104
  179.8 101.1 %while.31 = (s32[]{:T(128)}, f32[128,4096]{1,0:T(8,128)}, f32[128,2048]{1,0:T(8,128)S(1)}, s32[]{:T(128)}, s32[]{:T(128)}, /*index=5*/s32[]{:T(128)}, s32[]{:T(128)}) while((s32[]{:T(128)}, f32[128,4096]{1,0:T(8,128)}, f32[128,2048]{1,0:T(8,128)S(1)}, s32[]{:T(128)}, s32[]{:T(128)}, /*index=5*/s32[]{:T(128)}, s32[]{:T(128)}) %tuple.92), condition=%wide.region_9.10_spmd, body=%wide.region_8.9_spmd.sunk | while | flops 1619592704 | bytes 10760323 | solution.py:52
  179.8 8.3 %fusion.51 = (f32[512,1024]{1,0:T(8,128)S(1)}, f32[512,1024]{1,0:T(8,128)S(1)}) fusion(s32[512]{0:T(512)S(1)} %iota_add_fusion.8, s32[1024]{0:T(1024)S(1)} %iota_add_fusion.9), kind=kLoop, calls=%fused_computation.22.clone.1 | loop fusion | flops 7864320 | bytes 4200448 | tf_op jit(solution)/shard_map/while/body/eval_jaxpr/cos | solution.py:15
  192.4 8.3 %fusion.51 = (f32[512,1024]{1,0:T(8,128)S(1)}, f32[512,1024]{1,0:T(8,128)S(1)}) fusion(s32[512]{0:T(512)S(1)} %iota_add_fusion.8, s32[1024]{0:T(1024)S(1)} %iota_add_fusion.9), kind=kLoop, calls=%fused_computation.22.clone.1 | loop fusion | flops 7864320 | bytes 4200448 | tf_op jit(solution)/shard_map/while/body/eval_jaxpr/cos | solution.py:15
  205.1 8.3 %fusion.51 = (f32[512,1024]{1,0:T(8,128)S(1)}, f32[512,1024]{1,0:T(8,128)S(1)}) fusion(s32[512]{0:T(512)S(1)} %iota_add_fusion.8, s32[1024]{0:T(1024)S(1)} %iota_add_fusion.9), kind=kLoop, calls=%fused_computation.22.clone.1 | loop fusion | flops 7864320 | bytes 4200448 | tf_op jit(solution)/shard_map/while/body/eval_jaxpr/cos | solution.py:15
  217.7 8.3 %fusion.51 = (f32[512,1024]{1,0:T(8,128)S(1)}, f32[512,1024]{1,0:T(8,128)S(1)}) fusion(s32[512]{0:T(512)S(1)} %iota_add_fusion.8, s32[1024]{0:T(1024)S(1)} %iota_add_fusion.9), kind=kLoop, calls=%fused_computation.22.clone.1 | loop fusion | flops 7864320 | bytes 4200448 | tf_op jit(solution)/shard_map/while/body/eval_jaxpr/cos | solution.py:15
  230.4 8.3 %fusion.51 = (f32[512,1024]{1,0:T(8,128)S(1)}, f32[512,1024]{1,0:T(8,128)S(1)}) fusion(s32[512]{0:T(512)S(1)} %iota_add_fusion.8, s32[1024]{0:T(1024)S(1)} %iota_add_fusion.9), kind=kLoop, calls=%fused_computation.22.clone.1 | loop fusion | flops 7864320 | bytes 4200448 | tf_op jit(solution)/shard_map/while/body/eval_jaxpr/cos | solution.py:15
  243.0 8.3 %fusion.51 = (f32[512,1024]{1,0:T(8,128)S(1)}, f32[512,1024]{1,0:T(8,128)S(1)}) fusion(s32[512]{0:T(512)S(1)} %iota_add_fusion.8, s32[1024]{0:T(1024)S(1)} %iota_add_fusion.9), kind=kLoop, calls=%fused_computation.22.clone.1 | loop fusion | flops 7864320 | bytes 4200448 | tf_op jit(solution)/shard_map/while/body/eval_jaxpr/cos | solution.py:15
  255.6 8.3 %fusion.51 = (f32[512,1024]{1,0:T(8,128)S(1)}, f32[512,1024]{1,0:T(8,128)S(1)}) fusion(s32[512]{0:T(512)S(1)} %iota_add_fusion.8, s32[1024]{0:T(1024)S(1)} %iota_add_fusion.9), kind=kLoop, calls=%fused_computation.22.clone.1 | loop fusion | flops 7864320 | bytes 4200448 | tf_op jit(solution)/shard_map/while/body/eval_jaxpr/cos | solution.py:15
  268.3 8.3 %fusion.51 = (f32[512,1024]{1,0:T(8,128)S(1)}, f32[512,1024]{1,0:T(8,128)S(1)}) fusion(s32[512]{0:T(512)S(1)} %iota_add_fusion.8, s32[1024]{0:T(1024)S(1)} %iota_add_fusion.9), kind=kLoop, calls=%fused_computation.22.clone.1 | loop fusion | flops 7864320 | bytes 4200448 | tf_op jit(solution)/shard_map/while/body/eval_jaxpr/cos | solution.py:15
  285.1 6.5 %all-to-all-done.2 = f32[8,1,32]{2,1,0:T(1,128)S(1)} async-done(((f32[8,1,32]{2,1,0:T(1,128)}), f32[8,1,32]{2,1,0:T(1,128)S(1)}, u32[]{:S(2)}, u32[]{:S(2)}) %all-to-all-start.2) | async-done | bytes 1056 | tf_op jit(solution)/shard_map/all_to_all | solution.py:139
  294.6 16.6 %reduce-scatter.2.cloned.1.call-done = f32[32,4096]{1,0:T(8,128)} async-done(((f32[128,4096]{1,0:T(8,128)}), f32[32,4096]{1,0:T(8,128)}) %reduce-scatter.2.cloned.1.call-update) | async-done | bytes 524304 | tf_op jit(solution)/shard_map/reduce_scatter | solution.py:150
  (121 shorter events, 92.1 us)
Async XLA Ops:
  12.6 95.5 %all-to-all-start = ((s32[8,32,2]{1,2,0:T(2,128)}), s32[8,32,2]{1,2,0:T(2,128)S(1)}, u32[]{:S(2)}, u32[]{:S(2)}) async-start(s32[8,32,2]{1,2,0:T(2,128)} %pad_add_fusion), calls=%async_computation | async-start | bytes 16384 | tf_op jit(solution)/shard_map/all_to_all | solution.py:131
  19.9 84.7 %copy-start = (s32[16]{0:T(128)S(1)}, s32[16]{0:T(128)}, u32[]{:S(2)}) copy-start(s32[16]{0:T(128)} %param.11) | copy-start | bytes 196
  108.0 65.9 %all-to-all-start.1 = ((f32[8,32,2048]{2,1,0:T(8,128)}), f32[8,32,2048]{2,1,0:T(8,128)}, u32[]{:S(2)}, u32[]{:S(2)}) async-start(f32[8,32,2048]{2,1,0:T(8,128)} %bitcast.8), calls=%async_computation.1 | async-start | bytes 4194304 | tf_op jit(solution)/shard_map/all_to_all | solution.py:130
  114.0 197.2 %reduce-scatter.2.cloned.1.call-start = ((), (), s32[]{:S(2)}) async-start(), calls=%async_computation.4 | async-start | bytes 2621440 | tf_op jit(solution)/shard_map/reduce_scatter | solution.py:150
  115.0 19.5 %collective-permute-start = (f32[16,2048]{1,0:T(8,128)S(1)}, f32[16,2048]{1,0:T(8,128)S(1)}, u32[]{:S(2)}, u32[]{:S(2)}) collective-permute-start(f32[16,2048]{1,0:T(8,128)S(1)} %select_select_fusion), channel_id=1, source_target_pairs={{0,4},{4,0},{8,12},{12,8},{16,20},{20,16},{24,28},{28,24},{1,5},{5... | collective-permute-start | bytes 393224 | tf_op jit(solution)/shard_map/ppermute | solution.py:104
  134.5 16.2 %collective-permute-start.1 = (f32[16,2048]{1,0:T(8,128)S(1)}, f32[16,2048]{1,0:T(8,128)S(1)}, u32[]{:S(2)}, u32[]{:S(2)}) collective-permute-start(f32[16,2048]{1,0:T(8,128)S(1)} %fusion.42), channel_id=1, source_target_pairs={{0,8},{4,12},{8,0},{12,4},{16,24},{20,28},{24,16},{28,20},{1,9},{5... | collective-permute-start | bytes 393224 | tf_op jit(solution)/shard_map/ppermute | solution.py:104
  150.7 16.6 %collective-permute-start.2 = (f32[16,2048]{1,0:T(8,128)S(1)}, f32[16,2048]{1,0:T(8,128)S(1)}, u32[]{:S(2)}, u32[]{:S(2)}) collective-permute-start(f32[16,2048]{1,0:T(8,128)S(1)} %add.251), channel_id=1, source_target_pairs={{0,16},{4,20},{8,24},{12,28},{16,0},{20,4},{24,8},{28,12},{1,17},{... | collective-permute-start | bytes 393224 | tf_op jit(solution)/shard_map/ppermute | solution.py:104
  281.5 10.1 %all-to-all-start.2 = ((f32[8,1,32]{2,1,0:T(1,128)}), f32[8,1,32]{2,1,0:T(1,128)S(1)}, u32[]{:S(2)}, u32[]{:S(2)}) async-start(f32[8,1,32]{2,1,0:T(1,128)} %bitcast.11), calls=%async_computation.3 | async-start | bytes 8192 | tf_op jit(solution)/shard_map/all_to_all | solution.py:139
Sparse Core Ops, SparseCore 0:
  281.0 30.2 reduce-scatter.1
